TPU v7x, 32 devices: a whole 2x2x4 slice. The times are simulated.
32 devices in a mesh: ctx: 4 (over z), pipe: 2 (over x), tp: 4 (over y, core).
Axes of the slice: x: 2, y: 2, z: 4, core: 2. Of those that a mesh axis runs over, the one named last changes fastest.
Arguments:
- upstream: bfloat16 [2, 512, 2688], P('pipe', 'ctx', 'tp'), may hold values from -6 to 6
- saved_input: bfloat16 [2, 512, 2688], P('pipe', 'ctx', 'tp'), may hold values from -0.59765625 to 0.59765625
- inv_rms: float32 [2, 512], P('pipe', 'ctx'), may hold values from 2 to 20
- norm_gain: float32 [2, 2688], P('pipe', 'tp'), may hold values from 0.1 to 1.9
- query_proj: bfloat16 [2, 512, 2048], P('pipe', 'ctx', 'tp'), may hold values from -14 to 14
- key_proj: bfloat16 [2, 512, 1024], P('pipe', 'ctx', 'tp'), may hold values from -5.2 to 5.2
- stored_value_rows: bfloat16 [2, 512, 1024], P('pipe', 'ctx', 'tp'), may hold values from -6 to 6
- attn_out: bfloat16 [2, 512, 2048], P('pipe', 'ctx', 'tp'), may hold values from -6 to 6
- w_query: bfloat16 [2, 2688, 2048], P('pipe', None, 'tp'), may hold values from -0.125 to 0.125
- key_projection_weight: bfloat16 [2, 2688, 1024], P('pipe', None, 'tp'), may hold values from -0.125 to 0.125
- value_projection_weight: bfloat16 [2, 2688, 1024], P('pipe', None, 'tp'), may hold values from -0.125 to 0.125
- w_out: bfloat16 [2, 2048, 2688], P('pipe', 'tp'), may hold values from -0.125 to 0.125
- seq_lengths: int32 [2], P('pipe'), may hold values from 256 to 512, as said below
Outputs:
- next_grad: bfloat16 [2, 512, 2688], P('pipe', 'ctx', 'tp')
Inputs may be any that keep to these rules, and one draw needn't show every extreme that they name: `seq_lengths`: valid tokens come first in each sequence; at least one section's sequence has all 512 tokens valid.
All inputs are finite; a program needn't handle non-finite values.
Results may differ from a plain program's by a relative error of at most 0.0062.
Values may be sent and summed in bfloat16 or wider, within the bound.
A program may use at most 64 MiB of HBM per device.

v0:
```python
import jax
import jax.numpy as jnp
from jax import lax
from jax.sharding import PartitionSpec as P

MODEL_WIDTH = 2688
QUERY_HEADS = 16
KEY_VALUE_HEADS = 8
HEAD_SIZE = 128
WINDOW = 1024
QUERY_SCALAR = 168


NEG_FILL = -1e30
CONTRACT_LAST = (((1,), (1,)), ((), ()))


def shifted(value, axis, steps):
    count = lax.axis_size(axis)
    leading, last = (max(0, -steps), min(count, count - steps))
    return lax.ppermute(value, axis, [(source, source + steps) for source in range(leading, last)])


def from_behind(block, axis, distance):
    devices = range(lax.axis_size(axis))
    route = [((i - distance) % len(devices), i) for i in devices]
    return lax.ppermute(block, axis, route)


def window_mask(pos_query, pos_key, length):
    later = pos_query[:, None] - pos_key[None, :]
    inside = (later >= 0) & (later < WINDOW) & (pos_key[None, :] >= 0)
    return inside & (pos_key[None, :] < length) & (pos_query[:, None] < length)


def score_grads(
    query_head_rows, output_grad_heads, value_head_rows, weights, output_dot_grad, score_scale
):
    dprob = jnp.einsum(
        "tgrd,kgd->grtk", output_grad_heads, value_head_rows, preferred_element_type=jnp.float32
    )
    dscore = (weights * (dprob - output_dot_grad[..., None])).astype(jnp.bfloat16)
    weights_low = weights.astype(jnp.bfloat16)
    key_gradient = (
        jnp.einsum("grtk,tgrd->kgd", dscore, query_head_rows, preferred_element_type=jnp.float32)
        * score_scale
    )
    value_gradient = jnp.einsum(
        "grtk,tgrd->kgd", weights_low, output_grad_heads, preferred_element_type=jnp.float32
    )
    return (dscore, key_gradient, value_gradient)


def project(grad_low, weight):
    return lax.dot_general(grad_low, weight, CONTRACT_LAST, preferred_element_type=jnp.float32)


def per_device(
    upstream,
    saved_input,
    inv_rms,
    norm_gain,
    query_proj,
    key_proj,
    stored_value_rows,
    attn_out,
    w_query,
    key_projection_weight,
    value_projection_weight,
    w_out,
    seq_lengths,
):
    grad_in = upstream[0]
    block_row_count = grad_in.shape[0]
    queries = query_proj[0]
    key_local = key_proj[0]
    value_local = stored_value_rows[0]
    out_local = attn_out[0]
    out_weight = w_out[0]
    length = seq_lengths[0]
    kv_heads = key_local.shape[1] // HEAD_SIZE
    query_group_width = QUERY_HEADS // KEY_VALUE_HEADS
    score_scale = QUERY_SCALAR ** (-0.5)
    grad_out = lax.dot_general(
        lax.all_gather(grad_in, "tp", axis=1, tiled=True),
        out_weight,
        CONTRACT_LAST,
        preferred_element_type=jnp.float32,
    ).astype(jnp.bfloat16)
    ctx_count = lax.axis_size("ctx")
    reach = (WINDOW - 2 + block_row_count) // block_row_count
    steps_back = min(reach, ctx_count - 1)
    anchor_row = lax.axis_index("ctx") * block_row_count
    columns = key_local.shape[1]
    key_window = key_local
    value_window = value_local
    width = 1
    while width < reach + 1 and width < ctx_count:
        needed = min(width, reach + 1 - width)
        got_key, got_value = shifted(
            (key_window[-needed * block_row_count :], value_window[-needed * block_row_count :]),
            "ctx",
            width,
        )
        key_window = jnp.concatenate([got_key, key_window], axis=0)
        value_window = jnp.concatenate([got_value, value_window], axis=0)
        width = width + needed
    missing = (reach + 1 - width) * block_row_count
    if missing > 0:
        key_window = jnp.concatenate(
            [jnp.zeros((missing, columns), key_local.dtype), key_window], axis=0
        )
        value_window = jnp.concatenate(
            [jnp.zeros((missing, columns), value_local.dtype), value_window], axis=0
        )
    key_total_count = (reach + 1) * block_row_count
    pos_query = anchor_row + lax.iota(jnp.int32, block_row_count)
    pos_key = anchor_row - reach * block_row_count + lax.iota(jnp.int32, key_total_count)
    allowed = window_mask(pos_query, pos_key, length)
    live_rows = pos_query < length
    query_head_rows = queries.reshape(block_row_count, kv_heads, query_group_width, HEAD_SIZE)
    output_grad_heads = grad_out.reshape(block_row_count, kv_heads, query_group_width, HEAD_SIZE)
    output_heads = out_local.reshape(block_row_count, kv_heads, query_group_width, HEAD_SIZE)
    key_head_rows = key_window.reshape(key_total_count, kv_heads, HEAD_SIZE)
    value_head_rows = value_window.reshape(key_total_count, kv_heads, HEAD_SIZE)
    scores = (
        jnp.einsum(
            "tgrd,kgd->grtk", query_head_rows, key_head_rows, preferred_element_type=jnp.float32
        )
        * score_scale
    )
    scores = jnp.where(allowed, scores, NEG_FILL)
    top_score = jnp.max(scores, axis=-1)
    raised = jnp.where(allowed, jnp.exp(scores - top_score[..., None]), 0.0)
    row_total = jnp.sum(raised, axis=-1)
    weights = raised / jnp.where(live_rows[:, None], row_total[..., None], 1.0)
    output_dot_grad = jnp.einsum(
        "uhap,uhap->hau", output_grad_heads, output_heads, preferred_element_type=jnp.float32
    )
    dscore, key_gradient, value_gradient = score_grads(
        query_head_rows, output_grad_heads, value_head_rows, weights, output_dot_grad, score_scale
    )
    query_gradient = (
        (
            jnp.einsum("grtk,kgd->tgrd", dscore, key_head_rows, preferred_element_type=jnp.float32)
            * score_scale
        )
        .astype(jnp.bfloat16)
        .reshape(block_row_count, -1)
    )
    key_gradient = key_gradient.reshape(key_total_count, columns)
    value_gradient = value_gradient.reshape(key_total_count, columns)
    own_key = key_gradient[reach * block_row_count :]
    own_value = value_gradient[reach * block_row_count :]
    for distance in range(1, steps_back + 1):
        lower = (reach - distance) * block_row_count
        got_key, got_value = shifted(
            (
                key_gradient[lower : lower + block_row_count],
                value_gradient[lower : lower + block_row_count],
            ),
            "ctx",
            -distance,
        )
        own_key = own_key + got_key
        own_value = own_value + got_value
    key_low = own_key.astype(jnp.bfloat16)
    value_low = own_value.astype(jnp.bfloat16)
    normed_grad = (
        project(query_gradient, w_query[0])
        + project(key_low, key_projection_weight[0])
        + project(value_low, value_projection_weight[0])
    )
    coupling = (
        jnp.einsum("tc,tc->t", query_gradient, queries, preferred_element_type=jnp.float32)
        + jnp.einsum("tc,tc->t", key_low, key_local, preferred_element_type=jnp.float32)
        + jnp.einsum("tc,tc->t", value_low, value_local, preferred_element_type=jnp.float32)
    )
    tp_count = lax.axis_size("tp")
    coupling_cols = jnp.broadcast_to(coupling[:, None], (block_row_count, tp_count))
    normed_share, coupling_sum = (
        lax.psum_scatter(normed_grad, "tp", scatter_dimension=1, tiled=True),
        lax.psum_scatter(coupling_cols, "tp", scatter_dimension=1, tiled=True),
    )
    gain_shard = norm_gain[0]
    scale_rows = inv_rms[0][:, None]
    inputs = saved_input[0].astype(jnp.float32)
    dinput = (
        grad_in.astype(jnp.float32)
        + scale_rows
        * (gain_shard[None, :] * normed_share - inputs * scale_rows * coupling_sum / MODEL_WIDTH)
    ).astype(jnp.bfloat16)
    passed = from_behind(dinput, "pipe", -1)
    return passed[None]


def solution(mesh):
    placed = (
        P("pipe", "ctx", "tp"),
        P("pipe", "ctx", "tp"),
        P("pipe", "ctx"),
        P("pipe", "tp"),
        P("pipe", "ctx", "tp"),
        P("pipe", "ctx", "tp"),
        P("pipe", "ctx", "tp"),
        P("pipe", "ctx", "tp"),
        P("pipe", None, "tp"),
        P("pipe", None, "tp"),
        P("pipe", None, "tp"),
        P("pipe", "tp", None),
        P("pipe"),
    )
    return jax.shard_map(
        per_device, mesh=mesh, in_specs=placed, out_specs=P("pipe", "ctx", "tp"), check_vma=False
    )
```

profile of v0, /device:TPU:0, one launch (start us, length us, event | category | flops | bytes accessed | tf_op | source)
XLA Modules:
  0.0 119.7 jit_solution(4162395001396861791)
XLA Ops:
  6.5 1.1 copy.40
  7.6 5.0 %collective-permute-start = (bf16[128,256]{0,1:T(8,128)(2,1)S(1)}, bf16[128,256]{0,1:T(8,128)(2,1)S(1)}, u32[]{:S(2)}, u32[]{:S(2)}) collective-permute-start(bf16[128,256]{0,1:T(8,128)(2,1)S(1)} %bitcast.140), channel_id=1, source_target_pairs={{0,8},{8,16},{16,24},{1,9},{9,17},{17,25},{2,10},{10,18},{18,26},{... | collective-permute-start | bytes 196616 | tf_op jit(solution)/shard_map/ppermute | solution.py:21
  12.6 1.0 copy.46
  13.6 3.5 %collective-permute-start.2 = (bf16[128,256]{0,1:T(8,128)(2,1)S(1)}, bf16[128,256]{0,1:T(8,128)(2,1)S(1)}, u32[]{:S(2)}, u32[]{:S(2)}) collective-permute-start(bf16[128,256]{0,1:T(8,128)(2,1)S(1)} %bitcast.137), channel_id=1, source_target_pairs={{0,8},{8,16},{16,24},{1,9},{9,17},{17,25},{2,10},{10,18},{18,26},{... | collective-permute-start | bytes 196616 | tf_op jit(solution)/shard_map/ppermute | solution.py:21
  17.8 8.3 %all-gather = bf16[1,128,2688]{1,2,0:T(8,128)(2,1)S(1)} all-gather(bf16[1,128,672]{1,2,0:T(8,128)(2,1)} %param.13), channel_id=2, replica_groups=mesh['ctx'=4,'pipe'=2,'tp'=4] {'tp'}, dimensions={2}, use_global_device_ids=true | all-gather | bytes 860160 | tf_op jit(solution)/shard_map/all_gather | solution.py:85
  26.1 1.9 %fusion.31 = pred[128,1152]{0,1:T(8,128)(4,1)} fusion(s32[1152]{0:T(1024)S(1)} %iota_add_fusion, s32[128]{0:T(128)S(1)} %iota_add_fusion.1, pred[1152]{0:T(1024)(128)(4,1)S(1)} %get-tuple-element.19, pred[1152]{0:T(1024)(128)(4,1)S(1)} %get-tuple-element.20, pred[128]{0:T(512)(128)(4,1)S(1)} %broadcast_compare_fusion), kind=kLoop, calls=%fused_computation.41 | loop fusion | flops 1032192 | bytes 155008 | tf_op jit(solution)/shard_map/and | solution.py:33
  28.0 2.9 %fusion.19 = bf16[128,512]{1,0:T(8,128)(2,1)S(1)} fusion(bf16[1,512,2688]{2,1,0:T(8,128)(2,1)} %param.24, bf16[1,128,2688]{1,2,0:T(8,128)(2,1)S(1)} %all-gather), kind=kOutput, calls=%fused_computation.27 | convolution fusion | flops 352387072 | bytes 3571712 | tf_op jit(solution)/shard_map/dot_general | solution.py:84
  31.6 3.6 %collective-permute-start.1 = (bf16[256,256]{0,1:T(8,128)(2,1)}, bf16[256,256]{0,1:T(8,128)(2,1)}, u32[]{:S(2)}, u32[]{:S(2)}) collective-permute-start(bf16[256,256]{0,1:T(8,128)(2,1)} %pad_maximum_fusion), channel_id=1, source_target_pairs={{0,16},{8,24},{1,17},{9,25},{2,18},{10,26},{3,19},{11,27},{4,20},{... | collective-permute-start | bytes 393224 | tf_op jit(solution)/shard_map/ppermute | solution.py:21
  36.7 0.7 copy.50
  37.5 0.7 copy.43
  38.9 1.3 %collective-permute-start.3 = (bf16[256,256]{0,1:T(8,128)(2,1)}, bf16[256,256]{0,1:T(8,128)(2,1)S(1)}, u32[]{:S(2)}, u32[]{:S(2)}) collective-permute-start(bf16[256,256]{0,1:T(8,128)(2,1)} %pad_maximum_fusion.1), channel_id=1, source_target_pairs={{0,16},{8,24},{1,17},{9,25},{2,18},{10,26},{3,19},{11,27},{4,20},{... | collective-permute-start | bytes 393224 | tf_op jit(solution)/shard_map/ppermute | solution.py:21
  40.2 0.7 copy.49
  40.9 1.0 copy.42
  42.0 3.6 %fusion.64 = (f32[2,2,128]{2,1,0:T(2,128)S(1)}, f32[2,2,128,1152]{2,3,1,0:T(8,128)}) fusion(bf16[128,2,2,128]{0,3,2,1:T(8,128)(2,1)S(1)} %bitcast.144, pred[128,1152]{0,1:T(8,128)(4,1)} %fusion.31, bf16[128,2,128]{2,0,1:T(8,128)(2,1)} %copy.44, bf16[128,2,128]{2,0,1:T(8,128)(2,1)} %copy.43, bf16[256,2,128]{2,0,1:T(8,128)(2,1)S(1)} %copy.42, ...), kind=kOutput, calls=%fused_computation.87 | convolution fusion | flops 156304512 | bytes 2904320 | tf_op jit(solution)/shard_map/sub | solution.py:134
  45.7 2.3 %convolution_bitcast_fusion.1 = f32[1152,2,128]{0,2,1:T(8,128)S(1)} fusion(bf16[128,2,2,128]{0,3,2,1:T(8,128)(2,1)S(1)} %copy.56, f32[2,2,128,1152]{2,3,1,0:T(8,128)} %get-tuple-element.18, f32[2,2,128]{2,1,0:T(2,128)S(1)} %broadcast_select_fusion), kind=kOutput, calls=%fused_computation.17 | convolution fusion | flops 152174592 | bytes 3672064 | tf_op jit(solution)/shard_map/grtk,tgrd->kgd/dot_general | solution.py:48
  50.3 1.3 %collective-permute-start.7 = (f32[128,256]{0,1:T(8,128)S(1)}, f32[128,256]{0,1:T(8,128)S(1)}, u32[]{:S(2)}, u32[]{:S(2)}) collective-permute-start(f32[128,256]{0,1:T(8,128)S(1)} %bitcast.152), channel_id=1, source_target_pairs={{8,0},{16,8},{24,16},{9,1},{17,9},{25,17},{10,2},{18,10},{26,18},{... | collective-permute-start | bytes 393224 | tf_op jit(solution)/shard_map/ppermute | solution.py:21
  51.6 1.3 %collective-permute-start.8 = (f32[128,256]{0,1:T(8,128)S(1)}, f32[128,256]{0,1:T(8,128)S(1)}, u32[]{:S(2)}, u32[]{:S(2)}) collective-permute-start(f32[128,256]{0,1:T(8,128)S(1)} %bitcast.151), channel_id=1, source_target_pairs={{16,0},{24,8},{17,1},{25,9},{18,2},{26,10},{19,3},{27,11},{20,4},{... | collective-permute-start | bytes 393224 | tf_op jit(solution)/shard_map/ppermute | solution.py:21
  53.0 1.3 %collective-permute-start.4 = (f32[128,256]{0,1:T(8,128)S(1)}, f32[128,256]{0,1:T(8,128)S(1)}, u32[]{:S(2)}, u32[]{:S(2)}) collective-permute-start(f32[128,256]{0,1:T(8,128)S(1)} %bitcast.155), channel_id=1, source_target_pairs={{8,0},{16,8},{24,16},{9,1},{17,9},{25,17},{10,2},{18,10},{26,18},{... | collective-permute-start | bytes 393224 | tf_op jit(solution)/shard_map/ppermute | solution.py:21
  54.3 1.3 %collective-permute-start.5 = (f32[128,256]{0,1:T(8,128)S(1)}, f32[128,256]{0,1:T(8,128)S(1)}, u32[]{:S(2)}, u32[]{:S(2)}) collective-permute-start(f32[128,256]{0,1:T(8,128)S(1)} %bitcast.154), channel_id=1, source_target_pairs={{16,0},{24,8},{17,1},{25,9},{18,2},{26,10},{19,3},{27,11},{20,4},{... | collective-permute-start | bytes 393224 | tf_op jit(solution)/shard_map/ppermute | solution.py:21
  55.6 1.3 %collective-permute-start.6 = (f32[128,256]{0,1:T(8,128)S(1)}, f32[128,256]{0,1:T(8,128)S(1)}, u32[]{:S(2)}, u32[]{:S(2)}) collective-permute-start(f32[128,256]{0,1:T(8,128)S(1)} %bitcast.153), channel_id=1, source_target_pairs={{24,0},{25,1},{26,2},{27,3},{28,4},{29,5},{30,6},{31,7}} | collective-permute-start | bytes 393224 | tf_op jit(solution)/shard_map/ppermute | solution.py:21
  56.9 0.9 fusion.9
  57.8 4.4 %collective-permute-done.4 = f32[128,256]{0,1:T(8,128)S(1)} collective-permute-done((f32[128,256]{0,1:T(8,128)S(1)}, f32[128,256]{0,1:T(8,128)S(1)}, u32[]{:S(2)}, u32[]{:S(2)}) %collective-permute-start.4) | collective-permute-done | bytes 131104 | tf_op jit(solution)/shard_map/ppermute | solution.py:21
  62.1 1.3 %collective-permute-start.9 = (f32[128,256]{0,1:T(8,128)S(1)}, f32[128,256]{0,1:T(8,128)S(1)}, u32[]{:S(2)}, u32[]{:S(2)}) collective-permute-start(f32[128,256]{0,1:T(8,128)S(1)} %bitcast.150), channel_id=1, source_target_pairs={{24,0},{25,1},{26,2},{27,3},{28,4},{29,5},{30,6},{31,7}} | collective-permute-start | bytes 393224 | tf_op jit(solution)/shard_map/ppermute | solution.py:21
  63.4 14.3 %collective-permute-done.5 = f32[128,256]{0,1:T(8,128)S(1)} collective-permute-done((f32[128,256]{0,1:T(8,128)S(1)}, f32[128,256]{0,1:T(8,128)S(1)}, u32[]{:S(2)}, u32[]{:S(2)}) %collective-permute-start.5) | collective-permute-done | bytes 131104 | tf_op jit(solution)/shard_map/ppermute | solution.py:21
  78.4 0.7 copy-done.2
  79.1 1.6 %convolution_add_fusion = f32[128,2688]{0,1:T(8,128)} fusion(f32[128,2688]{0,1:T(8,128)S(1)} %convolution_add_fusion.1, bf16[128,256]{0,1:T(8,128)(2,1)S(1)} %get-tuple-element.8, bf16[1,2688,256]{2,1,0:T(8,128)(2,1)S(1)} %copy-done.2), kind=kOutput, calls=%fused_computation.2 | convolution fusion | flops 176504832 | bytes 4194304 | tf_op jit(solution)/shard_map/dot_general | solution.py:55
  82.2 1.0 multiply_reduce_fusion
  83.2 5.9 %all-reduce = f32[128,4]{0,1:T(4,128)S(1)} all-reduce(f32[128,4]{0,1:T(4,128)S(1)} %broadcast_in_dim.43), channel_id=4, replica_groups=mesh['ctx'=4,'pipe'=2,'tp'=4] {'tp'}, use_global_device_ids=true, to_apply=%region_3.4.clone | all-reduce | flops 512 | bytes 4096
  89.8 15.2 %reduce-scatter.2.cloned.1.call-done = f32[128,672]{0,1:T(8,128)} async-done(((f32[128,2688]{0,1:T(8,128)}), f32[128,672]{0,1:T(8,128)}) %reduce-scatter.2.cloned.1.call-update) | async-done | bytes 344080 | tf_op jit(solution)/shard_map/reduce_scatter | solution.py:182
  105.0 1.2 fusion.37
  106.2 1.5 %collective-permute-start.10 = (bf16[128,672]{0,1:T(8,128)(2,1)S(1)}, bf16[128,672]{0,1:T(8,128)(2,1)S(1)}, u32[]{:S(2)}, u32[]{:S(2)}) collective-permute-start(bf16[128,672]{0,1:T(8,128)(2,1)S(1)} %fusion.37), channel_id=1, source_target_pairs={{4,0},{0,4},{5,1},{1,5},{6,2},{2,6},{7,3},{3,7},{12,8},{8,12},{13,... | collective-permute-start | bytes 516104 | tf_op jit(solution)/shard_map/ppermute | solution.py:27
  107.7 4.5 %collective-permute-done.10 = bf16[128,672]{0,1:T(8,128)(2,1)S(1)} collective-permute-done((bf16[128,672]{0,1:T(8,128)(2,1)S(1)}, bf16[128,672]{0,1:T(8,128)(2,1)S(1)}, u32[]{:S(2)}, u32[]{:S(2)}) %collective-permute-start.10) | collective-permute-done | bytes 172064 | tf_op jit(solution)/shard_map/ppermute | solution.py:27
  (70 shorter events, 8.8 us)
Async XLA Ops:
  6.5 50.3 %copy-start = (bf16[1,2688,512]{2,1,0:T(8,128)(2,1)S(1)}, bf16[1,2688,512]{2,1,0:T(8,128)(2,1)}, u32[]{:S(2)}) copy-start(bf16[1,2688,512]{2,1,0:T(8,128)(2,1)} %param.21) | copy-start | bytes 8257540
  6.5 98.4 %reduce-scatter.2.cloned.1.call-start = ((), (), s32[]{:S(2)}) async-start(), calls=%async_computation.1 | async-start | bytes 1720320 | tf_op jit(solution)/shard_map/reduce_scatter | solution.py:182
  7.6 23.3 %collective-permute-start = (bf16[128,256]{0,1:T(8,128)(2,1)S(1)}, bf16[128,256]{0,1:T(8,128)(2,1)S(1)}, u32[]{:S(2)}, u32[]{:S(2)}) collective-permute-start(bf16[128,256]{0,1:T(8,128)(2,1)S(1)} %bitcast.140), channel_id=1, source_target_pairs={{0,8},{8,16},{16,24},{1,9},{9,17},{17,25},{2,10},{10,18},{18,26},{... | collective-permute-start | bytes 196616 | tf_op jit(solution)/shard_map/ppermute | solution.py:21
  13.6 24.7 %collective-permute-start.2 = (bf16[128,256]{0,1:T(8,128)(2,1)S(1)}, bf16[128,256]{0,1:T(8,128)(2,1)S(1)}, u32[]{:S(2)}, u32[]{:S(2)}) collective-permute-start(bf16[128,256]{0,1:T(8,128)(2,1)S(1)} %bitcast.137), channel_id=1, source_target_pairs={{0,8},{8,16},{16,24},{1,9},{9,17},{17,25},{2,10},{10,18},{18,26},{... | collective-permute-start | bytes 196616 | tf_op jit(solution)/shard_map/ppermute | solution.py:21
  28.0 2.9 %copy-start.5 = (bf16[1,128,512]{2,1,0:T(8,128)(2,1)S(1)}, bf16[1,128,512]{2,1,0:T(8,128)(2,1)}, u32[]{:S(2)}) copy-start(bf16[1,128,512]{2,1,0:T(8,128)(2,1)} %param.20) | copy-start | bytes 393220
  30.8 5.7 %copy-start.4 = (bf16[1,128,512]{2,1,0:T(8,128)(2,1)S(1)}, bf16[1,128,512]{2,1,0:T(8,128)(2,1)}, u32[]{:S(2)}) copy-start(bf16[1,128,512]{2,1,0:T(8,128)(2,1)} %param.17) | copy-start | bytes 393220
  31.6 9.3 %collective-permute-start.1 = (bf16[256,256]{0,1:T(8,128)(2,1)}, bf16[256,256]{0,1:T(8,128)(2,1)}, u32[]{:S(2)}, u32[]{:S(2)}) collective-permute-start(bf16[256,256]{0,1:T(8,128)(2,1)} %pad_maximum_fusion), channel_id=1, source_target_pairs={{0,16},{8,24},{1,17},{9,25},{2,18},{10,26},{3,19},{11,27},{4,20},{... | collective-permute-start | bytes 393224 | tf_op jit(solution)/shard_map/ppermute | solution.py:21
  38.9 6.7 %collective-permute-start.3 = (bf16[256,256]{0,1:T(8,128)(2,1)}, bf16[256,256]{0,1:T(8,128)(2,1)S(1)}, u32[]{:S(2)}, u32[]{:S(2)}) collective-permute-start(bf16[256,256]{0,1:T(8,128)(2,1)} %pad_maximum_fusion.1), channel_id=1, source_target_pairs={{0,16},{8,24},{1,17},{9,25},{2,18},{10,26},{3,19},{11,27},{4,20},{... | collective-permute-start | bytes 393224 | tf_op jit(solution)/shard_map/ppermute | solution.py:21
  45.7 2.3 %copy-start.8 = (bf16[128,2,128]{2,0,1:T(8,128)(2,1)S(1)}, bf16[128,2,128]{2,0,1:T(8,128)(2,1)}, u32[]{:S(2)}) copy-start(bf16[128,2,128]{2,0,1:T(8,128)(2,1)} %copy.50) | copy-start | bytes 196612
  45.7 2.3 %copy-start.9 = (bf16[128,2,128]{2,0,1:T(8,128)(2,1)S(1)}, bf16[128,2,128]{2,0,1:T(8,128)(2,1)}, u32[]{:S(2)}) copy-start(bf16[128,2,128]{2,0,1:T(8,128)(2,1)} %copy.49) | copy-start | bytes 196612
  45.7 2.4 %copy-start.13 = (f32[2,2,128,1152]{2,3,1,0:T(8,128)S(1)}, f32[2,2,128,1152]{2,3,1,0:T(8,128)}, u32[]{:S(2)}) copy-start(f32[2,2,128,1152]{2,3,1,0:T(8,128)} %get-tuple-element.18) | copy-start | bytes 7077892
  48.7 0.8 copy-start.6
  48.7 0.9 copy-start.7
  50.3 28.0 %collective-permute-start.7 = (f32[128,256]{0,1:T(8,128)S(1)}, f32[128,256]{0,1:T(8,128)S(1)}, u32[]{:S(2)}, u32[]{:S(2)}) collective-permute-start(f32[128,256]{0,1:T(8,128)S(1)} %bitcast.152), channel_id=1, source_target_pairs={{8,0},{16,8},{24,16},{9,1},{17,9},{25,17},{10,2},{18,10},{26,18},{... | collective-permute-start | bytes 393224 | tf_op jit(solution)/shard_map/ppermute | solution.py:21
  51.6 26.7 %collective-permute-start.8 = (f32[128,256]{0,1:T(8,128)S(1)}, f32[128,256]{0,1:T(8,128)S(1)}, u32[]{:S(2)}, u32[]{:S(2)}) collective-permute-start(f32[128,256]{0,1:T(8,128)S(1)} %bitcast.151), channel_id=1, source_target_pairs={{16,0},{24,8},{17,1},{25,9},{18,2},{26,10},{19,3},{27,11},{20,4},{... | collective-permute-start | bytes 393224 | tf_op jit(solution)/shard_map/ppermute | solution.py:21
  53.0 9.2 %collective-permute-start.4 = (f32[128,256]{0,1:T(8,128)S(1)}, f32[128,256]{0,1:T(8,128)S(1)}, u32[]{:S(2)}, u32[]{:S(2)}) collective-permute-start(f32[128,256]{0,1:T(8,128)S(1)} %bitcast.155), channel_id=1, source_target_pairs={{8,0},{16,8},{24,16},{9,1},{17,9},{25,17},{10,2},{18,10},{26,18},{... | collective-permute-start | bytes 393224 | tf_op jit(solution)/shard_map/ppermute | solution.py:21
  54.3 23.4 %collective-permute-start.5 = (f32[128,256]{0,1:T(8,128)S(1)}, f32[128,256]{0,1:T(8,128)S(1)}, u32[]{:S(2)}, u32[]{:S(2)}) collective-permute-start(f32[128,256]{0,1:T(8,128)S(1)} %bitcast.154), channel_id=1, source_target_pairs={{16,0},{24,8},{17,1},{25,9},{18,2},{26,10},{19,3},{27,11},{20,4},{... | collective-permute-start | bytes 393224 | tf_op jit(solution)/shard_map/ppermute | solution.py:21
  55.6 22.1 %collective-permute-start.6 = (f32[128,256]{0,1:T(8,128)S(1)}, f32[128,256]{0,1:T(8,128)S(1)}, u32[]{:S(2)}, u32[]{:S(2)}) collective-permute-start(f32[128,256]{0,1:T(8,128)S(1)} %bitcast.153), channel_id=1, source_target_pairs={{24,0},{25,1},{26,2},{27,3},{28,4},{29,5},{30,6},{31,7}} | collective-permute-start | bytes 393224 | tf_op jit(solution)/shard_map/ppermute | solution.py:21
  56.9 20.9 %copy-start.1 = (bf16[1,2688,256]{2,1,0:T(8,128)(2,1)S(1)}, bf16[1,2688,256]{2,1,0:T(8,128)(2,1)}, u32[]{:S(2)}) copy-start(bf16[1,2688,256]{2,1,0:T(8,128)(2,1)} %param.22) | copy-start | bytes 4128772
  62.1 16.2 %collective-permute-start.9 = (f32[128,256]{0,1:T(8,128)S(1)}, f32[128,256]{0,1:T(8,128)S(1)}, u32[]{:S(2)}, u32[]{:S(2)}) collective-permute-start(f32[128,256]{0,1:T(8,128)S(1)} %bitcast.150), channel_id=1, source_target_pairs={{24,0},{25,1},{26,2},{27,3},{28,4},{29,5},{30,6},{31,7}} | collective-permute-start | bytes 393224 | tf_op jit(solution)/shard_map/ppermute | solution.py:21
  77.8 1.3 %copy-start.2 = (bf16[1,2688,256]{2,1,0:T(8,128)(2,1)S(1)}, bf16[1,2688,256]{2,1,0:T(8,128)(2,1)}, u32[]{:S(2)}) copy-start(bf16[1,2688,256]{2,1,0:T(8,128)(2,1)} %param.23) | copy-start | bytes 4128772
  80.7 0.7 copy-start.12
  80.7 1.2 %copy-start.10 = (f32[1,672]{1,0:T(1,128)S(1)}, f32[1,672]{1,0:T(1,128)}, u32[]{:S(2)}) copy-start(f32[1,672]{1,0:T(1,128)} %param.16) | copy-start | bytes 8068
  80.7 24.2 %copy-start.3 = (bf16[1,128,672]{1,2,0:T(8,128)(2,1)S(1)}, bf16[1,128,672]{1,2,0:T(8,128)(2,1)}, u32[]{:S(2)}) copy-start(bf16[1,128,672]{1,2,0:T(8,128)(2,1)} %param.13) | copy-start | bytes 516100
  80.7 24.2 %copy-start.11 = (f32[1,128]{1,0:T(1,128)S(1)}, f32[1,128]{1,0:T(1,128)}, u32[]{:S(2)}) copy-start(f32[1,128]{1,0:T(1,128)} %param.15) | copy-start | bytes 1540
  106.2 6.0 %collective-permute-start.10 = (bf16[128,672]{0,1:T(8,128)(2,1)S(1)}, bf16[128,672]{0,1:T(8,128)(2,1)S(1)}, u32[]{:S(2)}, u32[]{:S(2)}) collective-permute-start(bf16[128,672]{0,1:T(8,128)(2,1)S(1)} %fusion.37), channel_id=1, source_target_pairs={{4,0},{0,4},{5,1},{1,5},{6,2},{2,6},{7,3},{3,7},{12,8},{8,12},{13,... | collective-permute-start | bytes 516104 | tf_op jit(solution)/shard_map/ppermute | solution.py:27
Sparse Core Ops, SparseCore 0:
  80.9 24.0 reduce-scatter.1
where the time goes:
time: 120 us
  waiting for transfers between devices  38.4 us (32%)
  starting transfers between devices  22.6 us (19%)
  between operations  14.4 us (12%)
  blocking collectives  14.2 us (12%)
  matrix products  13.5 us (11%)
  local copies, waits for them, and re-layouts  10.5 us (9%)
  other arithmetic  6.11 us (5%)
    ppermute x10, starting transfers between devices, shifted(): lax.ppermute(value, axis, [(source, source + steps) for source in range(l...  21.1 us
    ppermute x10, waiting for transfers between devices, shifted(): lax.ppermute(value, axis, [(source, source + steps) for source in range(l...  18.7 us
    reduce_scatter x1, waiting for transfers between devices, per_device(): lax.psum_scatter(normed_grad, 'tp', scatter_dimension=1, tiled=True)  15.2 us
    all_gather x1, blocking collectives, per_device(): lax.all_gather(grad_in, 'tp', axis=1, tiled=True)  8.3 us
    unnamed x1, blocking collectives  5.9 us
    unnamed x33, local copies, waits for them, and re-layouts  5.29 us
    ppermute x1, waiting for transfers between devices, from_behind(): return lax.ppermute(block, axis, route)  4.49 us
    sub x1, matrix products, per_device(): raised = jnp.where(allowed, jnp.exp(scores - top_score[..., None]), 0.0)  3.58 us
  transfers between devices with their start and end apart: 12, of which 4 were waited for; matrix products, arithmetic and copies ran while one was open for 16% of the time, Pallas kernels for 0%

commit v1 on v0

v1 whole, which is shorter than its diff:
```python
import functools

import jax
import jax.numpy as jnp
from jax import lax
from jax.experimental import pallas as pl
from jax.experimental.pallas import tpu as pltpu
from jax.sharding import PartitionSpec as P

QUERY_HEADS = 16
KEY_VALUE_HEADS = 8
HEAD_SIZE = 128
WINDOW = 1024
QUERY_SCALAR = 168
NEG_FILL = -1e30
ROW_CHUNKS = 4
NT = (((1,), (1,)), ((), ()))
NN = (((1,), (0,)), ((), ()))
TN = (((0,), (0,)), ((), ()))
BF = jnp.bfloat16
F32 = jnp.float32


def dot(a, b, dims):
    return lax.dot_general(a, b, dims, preferred_element_type=F32)


def kernel(
    ctx_n,
    pipe_n,
    reach,
    up_h,
    xin_h,
    inv_h,
    gain_h,
    q_h,
    k_h,
    v_h,
    ao_h,
    wq_h,
    wk_h,
    wv_h,
    wo_h,
    len_h,
    out_h,
    gath,
    xin,
    inv,
    gain,
    q,
    kb,
    vb,
    ao,
    wq,
    wk,
    wv,
    wo,
    slen,
    dout,
    dos,
    qs,
    s,
    part_k,
    part_v,
    snd_k,
    snd_v,
    rcv_k,
    rcv_v,
    dq,
    pacc,
    rs_a,
    rs_ar,
    rs_b,
    rs_br,
    rs_c,
    rs_cr,
    res,
    lsem,
    k_s,
    k_r,
    v_s,
    v_r,
    ag_s,
    ag_r,
    dk_s,
    dk_r,
    dv_s,
    dv_r,
    rs_s,
    rs_rv,
    x_s,
    x_r,
):
    i = lax.axis_index("ctx")
    p = lax.axis_index("pipe")
    t = lax.axis_index("tp")
    partner = t + 1 - 2 * (t % 2)
    cross = (t + 2) % 4
    diag = 3 - t
    rows = q.shape[0]
    width = xin.shape[1]
    kv_heads = kb.shape[2] // HEAD_SIZE
    group = q.shape[1] // kb.shape[2]
    stacked = group * rows
    scale = QUERY_SCALAR ** (-0.5)
    model_width = width * 4

    def local(src, dst, n):
        c = pltpu.make_async_copy(src, dst, lsem.at[n])
        c.start()
        return c

    def remote(src, dst, ss, rs, dev):
        return pltpu.make_async_remote_copy(
            src_ref=src,
            dst_ref=dst,
            send_sem=ss,
            recv_sem=rs,
            device_id=dev,
            device_id_type=pl.DeviceIdType.MESH,
        )

    c_k = local(k_h, kb.at[0], 0)
    c_q = local(q_h, q, 1)
    c_len = local(len_h, slen, 2)
    c_up = local(up_h, gath.at[t], 3)
    c_v = local(v_h, vb.at[0], 4)
    c_wo = local(wo_h, wo, 5)
    c_ao = local(ao_h, ao, 6)
    c_wq = local(wq_h, wq, 7)
    c_wk = local(wk_h, wk, 8)
    c_wv = local(wv_h, wv, 9)
    c_xin = local(xin_h, xin, 10)
    c_inv = local(inv_h, inv, 11)
    c_gain = local(gain_h, gain, 12)

    barrier = pltpu.get_barrier_semaphore()

    def greet(dev):
        pl.semaphore_signal(
            barrier, inc=1, device_id=dev, device_id_type=pl.DeviceIdType.MESH
        )

    has_up = i + 1 < ctx_n
    has_down = i > 0

    @pl.when(has_up)
    def _():
        greet({"ctx": i + 1})

    @pl.when(has_down)
    def _():
        greet({"ctx": i - 1})

    greet({"tp": partner})
    greet({"tp": cross})
    expect = 2
    prev = (p + pipe_n - 1) % pipe_n
    if pipe_n > 1:
        greet({"pipe": prev})
        expect += 1
    if pipe_n > 2:
        greet({"pipe": (p + 1) % pipe_n})
        expect += 1
    pl.semaphore_wait(
        barrier, expect + jnp.where(has_up, 1, 0) + jnp.where(has_down, 1, 0)
    )

    up_dev = {"ctx": i + 1}
    down_dev = {"ctx": i - 1}

    def k_copy(d):
        src = k_h if d == 0 else kb.at[d]
        return remote(src, kb.at[d + 1], k_s.at[d], k_r.at[d + 1], up_dev)

    def v_copy(d):
        src = v_h if d == 0 else vb.at[d]
        return remote(src, vb.at[d + 1], v_s.at[d], v_r.at[d + 1], up_dev)

    ag_cross = remote(up_h, gath.at[t], ag_s.at[0], ag_r.at[0], {"tp": cross})
    ag_part = remote(up_h, gath.at[t], ag_s.at[1], ag_r.at[1], {"tp": partner})
    ag_fwd = remote(
        gath.at[cross], gath.at[cross], ag_s.at[2], ag_r.at[2], {"tp": partner}
    )
    ag_cross.start()

    @pl.when(has_up)
    def _():
        k_copy(0).start()
        v_copy(0).start()

    ag_part.start()

    c_len.wait()
    length = slen[0]
    key_i = lax.broadcasted_iota(jnp.int32, (rows, stacked), 0)
    qry_i = lax.broadcasted_iota(jnp.int32, (rows, stacked), 1) % rows
    later0 = qry_i - key_i
    pos_q = i * rows + qry_i
    live = pos_q < length

    def scores(d):
        later = later0 + d * rows
        pos_k = pos_q - later
        ok = (later >= 0) & (later < WINDOW) & (pos_k < length) & live
        for g in range(kv_heads):
            cols = slice(g * HEAD_SIZE, (g + 1) * HEAD_SIZE)
            sc = dot(kb[d, :, cols], qs[g], NT) * scale
            s[d, g] = jnp.where(ok, sc, NEG_FILL)

    c_q.wait()
    for g in range(kv_heads):
        for r in range(group):
            h = g * group + r
            qs[g, r * rows : (r + 1) * rows, :] = q[:, h * HEAD_SIZE : (h + 1) * HEAD_SIZE]
    c_k.wait()
    scores(0)

    def take(d):
        @pl.when(i >= d)
        def _():
            k_copy(d - 1).wait_recv()
            if d < reach:

                @pl.when(has_up)
                def _():
                    k_copy(d).start()

            scores(d)
            v_copy(d - 1).wait_recv()
            if d < reach:

                @pl.when(has_up)
                def _():
                    v_copy(d).start()

    if reach >= 1:
        take(1)
    ag_cross.wait_recv()
    ag_fwd.start()
    for d in range(2, reach + 1):
        take(d)

    ag_part.wait_recv()
    ag_fwd.wait_recv()
    c_up.wait()
    c_wo.wait()
    whole = jnp.concatenate([gath[n] for n in range(4)], axis=1)
    dout[...] = dot(whole, wo[...], NT).astype(BF)
    c_ao.wait()
    deltas = []
    for g in range(kv_heads):
        prods = []
        for r in range(group):
            h = g * group + r
            cols = slice(h * HEAD_SIZE, (h + 1) * HEAD_SIZE)
            grad = dout[:, cols]
            dos[g, r * rows : (r + 1) * rows, :] = grad
            prod = grad.astype(F32) * ao[:, cols].astype(F32)
            prods.append(jnp.sum(prod.T, axis=0, keepdims=True))
        deltas.append(jnp.concatenate(prods, axis=1))

    for d in range(1, reach + 1):

        @pl.when(i < d)
        def _():
            s[d] = jnp.full(s.shape[1:], NEG_FILL, F32)

    tops, inv_totals = [], []
    for g in range(kv_heads):
        top = jnp.max(s[0, g], axis=0, keepdims=True)
        for d in range(1, reach + 1):
            top = jnp.maximum(top, jnp.max(s[d, g], axis=0, keepdims=True))
        total = jnp.zeros((1, stacked), F32)
        for d in range(reach + 1):
            val = s[d, g]
            e = jnp.where(val > 0.5 * NEG_FILL, jnp.exp(val - top), 0.0)
            s[d, g] = e
            total = total + jnp.sum(e, axis=0, keepdims=True)
        inv_totals.append(1.0 / jnp.where(live[:1], total, 1.0))

    c_v.wait()

    def dk_copy(d):
        return remote(snd_k.at[d], rcv_k.at[d - 1], dk_s.at[d], dk_r.at[d - 1], down_dev)

    def dv_copy(d):
        return remote(snd_v.at[d], rcv_v.at[d - 1], dv_s.at[d], dv_r.at[d - 1], down_dev)

    dq[...] = jnp.zeros_like(dq)

    def first_of_chain(d):
        return i + 1 >= ctx_n if d < reach else i >= d

    def block(d):
        probs = []
        for g in range(kv_heads):
            cols = slice(g * HEAD_SIZE, (g + 1) * HEAD_SIZE)
            prob = s[d, g] * inv_totals[g]
            probs.append(prob)
            part_v[d, :, cols] = dot(prob.astype(BF), dos[g], NN)
        if d > 0:

            @pl.when(first_of_chain(d))
            def _():
                snd_v[d] = part_v[d].astype(BF)
                dv_copy(d).start()

        for g in range(kv_heads):
            cols = slice(g * HEAD_SIZE, (g + 1) * HEAD_SIZE)
            dprob = dot(vb[d, :, cols], dos[g], NT)
            ds = (probs[g] * (dprob - deltas[g])).astype(BF)
            part_k[d, :, cols] = dot(ds, qs[g], NN)
            dq[g] += dot(ds, kb[d, :, cols], TN)
        if d > 0:

            @pl.when(first_of_chain(d))
            def _():
                snd_k[d] = part_k[d].astype(BF)
                dk_copy(d).start()

    for d in range(reach, 0, -1):
        pl.when(i >= d)(functools.partial(block, d))
    block(0)

    coupling = jnp.zeros((rows, 1), F32)
    low = []
    for g in range(kv_heads):
        for r in range(group):
            h = g * group + r
            part = (dq[g, r * rows : (r + 1) * rows, :] * scale).astype(BF)
            low.append(part)
            coupling = coupling + jnp.sum(
                part.astype(F32) * q[:, h * HEAD_SIZE : (h + 1) * HEAD_SIZE].astype(F32),
                axis=1,
                keepdims=True,
            )
    dq_low = jnp.concatenate(low, axis=1)
    owners = (diag, cross, partner, t)

    def piece_rows(n):
        return pl.ds(pl.multiple_of(owners[n] * width, 32), width)

    def query_piece(n):
        pacc[n] = dot(dq_low, wq[piece_rows(n), :], NT)

    c_wq.wait()
    done = 0
    for d in range(reach - 1, 0, -1):

        @pl.when(has_up & (i >= d))
        def _():
            dv_copy(d + 1).wait_recv()
            snd_v[d] = (part_v[d] + rcv_v[d].astype(F32)).astype(BF)
            dv_copy(d).start()
            dk_copy(d + 1).wait_recv()
            snd_k[d] = (part_k[d] + rcv_k[d].astype(F32)).astype(BF)
            dk_copy(d).start()

        if done < 4:
            query_piece(done)
            done += 1
    while done < 4:
        query_piece(done)
        done += 1
    c_wk.wait()
    c_wv.wait()
    if reach >= 1:

        @pl.when(has_up)
        def _():
            dv_copy(1).wait_recv()
            part_v[0] += rcv_v[0].astype(F32)
            dk_copy(1).wait_recv()
            part_k[0] += rcv_k[0].astype(F32)

    dk_low = (part_k[0] * scale).astype(BF)
    dv_low = part_v[0].astype(BF)
    coupling = coupling + jnp.sum(
        dk_low.astype(F32) * kb[0].astype(F32) + dv_low.astype(F32) * vb[0].astype(F32),
        axis=1,
        keepdims=True,
    )

    def piece(n):
        sl = piece_rows(n)
        return pacc[n] + dot(dk_low, wk[sl, :], NT) + dot(dv_low, wv[sl, :], NT)

    tail = rs_a.shape[1] - width
    wide = jnp.broadcast_to(coupling, (rows, tail))
    chunk = rows // ROW_CHUNKS

    send_a = remote(rs_a, rs_ar, rs_s.at[0], rs_rv.at[0], {"tp": partner})
    send_c = remote(rs_c, rs_cr, rs_s.at[1], rs_rv.at[1], {"tp": partner})

    def b_copy(n):
        sl = pl.ds(n * chunk, chunk)
        return remote(
            rs_b.at[sl], rs_br.at[sl], rs_s.at[2 + n], rs_rv.at[2 + n], {"tp": cross}
        )

    def x_copy(n):
        sl = pl.ds(n * chunk, chunk)
        return remote(res.at[sl], out_h.at[sl], x_s.at[n], x_r.at[n], {"pipe": prev})

    rs_a[:, :width] = piece(0).astype(BF)
    rs_a[:, width:] = wide.astype(BF)
    send_a.start()
    pacc[1] = piece(1)
    send_a.wait_recv()
    for n in range(ROW_CHUNKS):
        sl = slice(n * chunk, (n + 1) * chunk)
        rs_b[sl, :width] = (pacc[1, sl] + rs_ar[sl, :width].astype(F32)).astype(BF)
        rs_b[sl, width:] = (wide[sl] + rs_ar[sl, width:].astype(F32)).astype(BF)
        b_copy(n).start()
    rs_c[:, :width] = piece(2).astype(BF)
    rs_c[:, width:] = wide.astype(BF)
    send_c.start()
    pacc[3] = piece(3)
    c_xin.wait()
    c_inv.wait()
    c_gain.wait()
    inv_col = jnp.broadcast_to(inv[...], (rows, rows)).T[:, :1]
    send_c.wait_recv()
    for n in range(ROW_CHUNKS):
        sl = slice(n * chunk, (n + 1) * chunk)
        b_copy(n).wait_recv()
        normed = pacc[3, sl] + rs_cr[sl, :width].astype(F32) + rs_br[sl, :width].astype(F32)
        coup = (
            coupling[sl]
            + rs_cr[sl, width : width + 1].astype(F32)
            + rs_br[sl, width : width + 1].astype(F32)
        )
        iv = inv_col[sl]
        upl = gath[t, sl, :].astype(F32)
        val = upl + iv * (
            gain[...] * normed - xin[sl, :].astype(F32) * (iv * coup / model_width)
        )
        res[sl, :] = val.astype(BF)
        if pipe_n > 1:
            x_copy(n).start()
        else:
            pltpu.make_async_copy(
                res.at[pl.ds(n * chunk, chunk)], out_h.at[pl.ds(n * chunk, chunk)], x_s.at[n]
            ).start()

    ag_cross.wait_send()
    ag_part.wait_send()
    ag_fwd.wait_send()
    for d in range(reach):

        @pl.when(has_up & (i >= d))
        def _():
            k_copy(d).wait_send()
            v_copy(d).wait_send()

    for d in range(1, reach + 1):

        @pl.when(i >= d)
        def _():
            dv_copy(d).wait_send()
            dk_copy(d).wait_send()

    send_a.wait_send()
    send_c.wait_send()
    for n in range(ROW_CHUNKS):
        b_copy(n).wait_send()
    for n in range(ROW_CHUNKS):
        if pipe_n > 1:
            x_copy(n).wait()
        else:
            pltpu.make_async_copy(
                res.at[pl.ds(n * chunk, chunk)], out_h.at[pl.ds(n * chunk, chunk)], x_s.at[n]
            ).wait()


def per_device(up, xin, inv, gain, q, k, v, ao, wq, wk, wv, wo, lens):
    ctx_n = lax.axis_size("ctx")
    pipe_n = lax.axis_size("pipe")
    tp_n = lax.axis_size("tp")
    assert tp_n == 4
    up, xin, q, k, v, ao = up[0], xin[0], q[0], k[0], v[0], ao[0]
    wq, wk, wv, wo = wq[0], wk[0], wv[0], wo[0]
    rows, width = up.shape
    reach = min((WINDOW - 2 + rows) // rows, ctx_n - 1)
    kv_cols, q_cols = k.shape[1], q.shape[1]
    kv_heads = kv_cols // HEAD_SIZE
    stacked = rows * (q_cols // kv_cols)
    pad = (width + 127) // 128 * 128
    if pad == width:
        pad += 128
    vm = pltpu.VMEM
    dma = pltpu.SemaphoreType.DMA
    blocks = reach + 1
    scratch = [
        vm((tp_n, rows, width), BF),
        vm((rows, width), BF),
        vm(inv.shape, F32),
        vm(gain.shape, F32),
        vm(q.shape, BF),
        vm((blocks, rows, kv_cols), BF),
        vm((blocks, rows, kv_cols), BF),
        vm(ao.shape, BF),
        vm(wq.shape, BF),
        vm(wk.shape, BF),
        vm(wv.shape, BF),
        vm(wo.shape, BF),
        pltpu.SMEM(lens.shape, jnp.int32),
        vm(q.shape, BF),
        vm((kv_heads, stacked, HEAD_SIZE), BF),
        vm((kv_heads, stacked, HEAD_SIZE), BF),
        vm((blocks, kv_heads, rows, stacked), F32),
        vm((blocks, rows, kv_cols), F32),
        vm((blocks, rows, kv_cols), F32),
        vm((blocks, rows, kv_cols), BF),
        vm((blocks, rows, kv_cols), BF),
        vm((blocks, rows, kv_cols), BF),
        vm((blocks, rows, kv_cols), BF),
        vm((kv_heads, stacked, HEAD_SIZE), F32),
        vm((tp_n, rows, width), F32),
    ]
    scratch += [vm((rows, pad), BF)] * 6
    scratch += [vm((rows, width), BF)]
    scratch += [dma((13,))]
    scratch += [dma((blocks,))] * 4
    scratch += [dma((3,))] * 2
    scratch += [dma((blocks,))] * 4
    scratch += [dma((2 + ROW_CHUNKS,))] * 2
    scratch += [dma((ROW_CHUNKS,))] * 2
    out = pl.pallas_call(
        functools.partial(kernel, ctx_n, pipe_n, reach),
        out_shape=jax.ShapeDtypeStruct((rows, width), BF),
        in_specs=[pl.BlockSpec(memory_space=pl.ANY)] * 13,
        out_specs=pl.BlockSpec(memory_space=pl.ANY),
        scratch_shapes=scratch,
        compiler_params=pltpu.CompilerParams(collective_id=0, has_side_effects=True),
        name="layer_backward",
    )(up, xin, inv, gain, q, k, v, ao, wq, wk, wv, wo, lens)
    return out[None]


def solution(mesh):
    placed = (
        P("pipe", "ctx", "tp"),
        P("pipe", "ctx", "tp"),
        P("pipe", "ctx"),
        P("pipe", "tp"),
        P("pipe", "ctx", "tp"),
        P("pipe", "ctx", "tp"),
        P("pipe", "ctx", "tp"),
        P("pipe", "ctx", "tp"),
        P("pipe", None, "tp"),
        P("pipe", None, "tp"),
        P("pipe", None, "tp"),
        P("pipe", "tp", None),
        P("pipe"),
    )
    return jax.shard_map(
        per_device, mesh=mesh, in_specs=placed, out_specs=P("pipe", "ctx", "tp"), check_vma=False
    )
```

time: 120 us -> 46.8 us (0.39)
  Pallas kernels: 0 us -> 40.7 us
  waiting for transfers between devices: 38.4 us -> 0 us
  starting transfers between devices: 22.6 us -> 0 us
  blocking collectives: 14.2 us -> 0 us
  between operations: 14.4 us -> 0.66 us
  matrix products: 13.5 us -> 0 us
  other arithmetic: 6.11 us -> 0 us
  local copies, waits for them, and re-layouts: 10.5 us -> 5.19 us
    pallas_call x0 -> x1, Pallas kernels: none -> 40.7 us  [per_device(): pl.pallas_call(functools.partial(kernel, ctx_n, pipe_n, reach), out_shape...]
    ppermute x11 -> x0, waiting for transfers between devices: 23.2 us -> none  [the longest x10 18.7 us: shifted(): lax.ppermute(value, axis, [(source, source + steps) for source in range(l...]
    ppermute x11 -> x0, starting transfers between devices: 22.6 us -> none  [the longest x10 21.1 us: shifted(): lax.ppermute(value, axis, [(source, source + steps) for source in range(l...]
    reduce_scatter x1 -> x0, waiting for transfers between devices: 15.2 us -> none  [per_device(): lax.psum_scatter(normed_grad, 'tp', scatter_dimension=1, tiled=True)]
    dot_general x8 -> x0, matrix products: 9.9 us -> none  [the longest x3 3.01 us: project(): lax.dot_general(grad_low, weight, CONTRACT_LAST, preferred_element_type=j...]
    all_gather x1 -> x0, blocking collectives: 8.3 us -> none  [per_device(): lax.all_gather(grad_in, 'tp', axis=1, tiled=True)]
    unnamed x1 -> x0, blocking collectives: 5.9 us -> none
    concatenate x8 -> x0, local copies, waits for them, and re-layouts: 4.1 us -> none  [the longest x5 2.5 us: per_device(): jnp.concatenate([jnp.zeros((missing, columns), key_local.dtype), key_wind...]
  transfers between devices with their start and end apart: 12 -> 0, of which waited for: 4 -> 0; matrix products, arithmetic and copies ran while one was open for 16% -> 0% of each run, Pallas kernels for 0% -> 0%
where the time goes in v1:
time: 46.8 us; the launch traced here: 46.6 us
  Pallas kernels  40.7 us (87%)
  local copies, waits for them, and re-layouts  5.19 us (11%)
  between operations  0.66 us (1%)
    pallas_call x1, Pallas kernels, per_device(): pl.pallas_call(functools.partial(kernel, ctx_n, pipe_n, reach), out_shape...  40.7 us
    unnamed x2, local copies, waits for them, and re-layouts  3.46 us
    broadcast_in_dim x1, local copies, waits for them, and re-layouts, per_device(): return out[None]  1.73 us

profile of v1, /device:TPU:0, one launch (start us, length us, event | category | flops | bytes accessed | tf_op | source)
XLA Modules:
  0.0 46.6 jit_solution(17437157243174320987)
XLA Ops:
  0.7 1.7 %copy.14 = bf16[1,128,672]{2,1,0:T(8,128)(2,1)} copy(bf16[1,128,672]{1,2,0:T(8,128)(2,1)} %param.13) | data formatting | bytes 344064 | tf_op args[0]
  2.4 1.7 %copy.15 = bf16[1,128,672]{2,1,0:T(8,128)(2,1)} copy(bf16[1,128,672]{1,2,0:T(8,128)(2,1)} %param.14) | data formatting | bytes 344064 | tf_op args[1]
  4.1 40.7 %layer_backward.1 = bf16[128,672]{1,0:T(8,128)(2,1)} custom-call(bf16[128,672]{1,0:T(8,128)(2,1)} %bitcast.16, bf16[128,672]{1,0:T(8,128)(2,1)} %bitcast.17, f32[1,128]{1,0:T(1,128)} %inv_h.1, f32[1,672]{1,0:T(1,128)} %gain_h.1, bf16[128,512]{1,0:T(8,128)(2,1)} %bitcast.18, bf16[128,256]{1,0:T(8,128)(2,1)} %bitcast.20, bf16[128,256]{1,0:T(8,128)(2,1)} %bitcast.21, ...), custom_call_target="tpu_custom_call" | custom-call | tf_op jit(solution)/shard_map/layer_backward/pallas_call | solution.py:530
  44.8 1.7 %copy.16 = bf16[1,128,672]{1,2,0:T(8,128)(2,1)} copy(bf16[1,128,672]{2,1,0:T(8,128)(2,1)} %bitcast.15) | data formatting | bytes 344064 | tf_op jit(solution)/shard_map/broadcast_in_dim | solution.py:539

commit v2 on v1

v2 whole, which is shorter than its diff:
```python
import functools

import jax
import jax.numpy as jnp
from jax import lax
from jax.experimental import pallas as pl
from jax.experimental.pallas import tpu as pltpu
from jax.sharding import PartitionSpec as P

QUERY_HEADS = 16
KEY_VALUE_HEADS = 8
HEAD_SIZE = 128
WINDOW = 1024
QUERY_SCALAR = 168
NEG_FILL = -1e30
GATHER_PARTS = 2
COUPLING_ROWS = 16
NT = (((1,), (1,)), ((), ()))
NN = (((1,), (0,)), ((), ()))
TN = (((0,), (0,)), ((), ()))
BF = jnp.bfloat16
F32 = jnp.float32


def chunk_count(width):
    for n in (6, 4, 3, 2):
        if width % (16 * n) == 0:
            return n
    return 1


def dot(a, b, dims):
    return lax.dot_general(a, b, dims, preferred_element_type=F32)


def kernel(
    ctx_n,
    pipe_n,
    reach,
    up_h,
    xin_h,
    inv_h,
    gain_h,
    q_h,
    k_h,
    v_h,
    ao_h,
    wq_h,
    wk_h,
    wv_h,
    wo_h,
    len_h,
    out_h,
    gath,
    xin,
    inv,
    gain,
    q,
    kb,
    vb,
    ao,
    wq,
    wk,
    wv,
    wo,
    slen,
    wo_cut,
    gain_col,
    ao_t,
    q_t,
    k_t,
    do_t,
    s,
    part_k,
    part_v,
    snd_k,
    snd_v,
    rcv_k,
    rcv_v,
    dq,
    pacc,
    rs_a,
    rs_ar,
    rs_b,
    rs_br,
    rs_c,
    rs_cr,
    res,
    lsem,
    k_s,
    k_r,
    v_s,
    v_r,
    ag_s,
    ag_r,
    dk_s,
    dk_r,
    dv_s,
    dv_r,
    rs_s,
    rs_rv,
    x_s,
    x_r,
):
    i = lax.axis_index("ctx")
    p = lax.axis_index("pipe")
    t = lax.axis_index("tp")
    partner = t + 1 - 2 * (t % 2)
    cross = (t + 2) % 4
    diag = 3 - t
    rows = q.shape[0]
    width = xin.shape[0]
    kv_heads = kb.shape[2] // HEAD_SIZE
    group = q.shape[1] // kb.shape[2]
    stacked = group * rows
    scale = QUERY_SCALAR ** (-0.5)
    model_width = width * 4
    chunks = chunk_count(width)
    chunk = width // chunks

    def local(src, dst, n):
        c = pltpu.make_async_copy(src, dst, lsem.at[n])
        c.start()
        return c

    def remote(src, dst, ss, rs, dev):
        return pltpu.make_async_remote_copy(
            src_ref=src,
            dst_ref=dst,
            send_sem=ss,
            recv_sem=rs,
            device_id=dev,
            device_id_type=pl.DeviceIdType.MESH,
        )

    barrier = pltpu.get_barrier_semaphore()

    def greet(dev):
        pl.semaphore_signal(
            barrier, inc=1, device_id=dev, device_id_type=pl.DeviceIdType.MESH
        )

    has_up = i + 1 < ctx_n
    has_down = i > 0

    @pl.when(has_up)
    def _():
        greet({"ctx": i + 1})

    @pl.when(has_down)
    def _():
        greet({"ctx": i - 1})

    greet({"tp": partner})
    greet({"tp": cross})
    expect = 2
    prev = (p + pipe_n - 1) % pipe_n
    if pipe_n > 1:
        greet({"pipe": prev})
        expect += 1
    if pipe_n > 2:
        greet({"pipe": (p + 1) % pipe_n})
        expect += 1

    c_k = local(k_h, kb.at[0], 0)
    c_q = local(q_h, q, 1)
    c_len = local(len_h, slen, 2)
    c_up = local(up_h, gath.at[t], 3)
    c_wo = local(wo_h, wo, 5)
    c_ao = local(ao_h, ao, 6)
    c_gain = local(gain_h, gain, 12)
    c_v = local(v_h, vb.at[0], 4)
    c_wq = local(wq_h, wq, 7)
    c_wk = local(wk_h, wk, 8)
    c_wv = local(wv_h, wv, 9)
    c_xin = local(xin_h, xin, 10)
    c_inv = local(inv_h, inv, 11)

    pl.semaphore_wait(
        barrier, expect + jnp.where(has_up, 1, 0) + jnp.where(has_down, 1, 0)
    )

    up_dev = {"ctx": i + 1}
    down_dev = {"ctx": i - 1}

    def k_copy(d):
        src = k_h if d == 0 else kb.at[d]
        return remote(src, kb.at[d + 1], k_s.at[d], k_r.at[d + 1], up_dev)

    def v_copy(d):
        src = v_h if d == 0 else vb.at[d]
        return remote(src, vb.at[d + 1], v_s.at[d], v_r.at[d + 1], up_dev)

    half = width // GATHER_PARTS

    def ag_cross(n):
        sl = pl.ds(n * half, half)
        return remote(up_h.at[sl], gath.at[t, sl], ag_s.at[n], ag_r.at[n], {"tp": cross})

    def ag_fwd(n):
        sl = pl.ds(n * half, half)
        m = GATHER_PARTS + n
        return remote(
            gath.at[cross, sl], gath.at[cross, sl], ag_s.at[m], ag_r.at[m], {"tp": partner}
        )

    own_slot = 2 * GATHER_PARTS
    ag_part = remote(
        up_h, gath.at[t], ag_s.at[own_slot], ag_r.at[own_slot], {"tp": partner}
    )
    for n in range(GATHER_PARTS):
        ag_cross(n).start()

    @pl.when(has_up)
    def _():
        k_copy(0).start()
        v_copy(0).start()

    ag_part.start()

    c_len.wait()
    length = slen[0]
    key_i = lax.broadcasted_iota(jnp.int32, (rows, stacked), 0)
    qry_i = lax.broadcasted_iota(jnp.int32, (rows, stacked), 1) % rows
    later0 = qry_i - key_i
    pos_q = i * rows + qry_i
    live = pos_q < length

    def head_cols(h):
        return slice(h * HEAD_SIZE, (h + 1) * HEAD_SIZE)

    def flip(x):
        return x.astype(F32).T

    def scores(d):
        later = later0 + d * rows
        pos_k = pos_q - later
        ok = (later >= 0) & (later < WINDOW) & (pos_k < length) & live
        for g in range(kv_heads):
            keys = kb[d, :, head_cols(g)]
            sc = dot(keys, q_t[g], NN) * scale
            s[d, g] = jnp.where(ok, sc, NEG_FILL)
            k_t[d, g] = flip(keys).astype(BF)

    c_q.wait()
    for g in range(kv_heads):
        for r in range(group):
            q_t[g, :, r * rows : (r + 1) * rows] = flip(q[:, head_cols(g * group + r)]).astype(BF)
    c_k.wait()
    scores(0)
    c_ao.wait()
    for h in range(kv_heads * group):
        ao_t[head_cols(h), :] = flip(ao[:, head_cols(h)])
    c_wo.wait()
    for n in range(4):
        wo_cut[n] = wo[:, n * width : (n + 1) * width]
    c_gain.wait()
    gain_col[...] = jnp.broadcast_to(gain[...], (rows, width)).T

    def take_k(d):
        @pl.when(i >= d)
        def _():
            k_copy(d - 1).wait_recv()
            if d < reach:

                @pl.when(has_up)
                def _():
                    k_copy(d).start()

            scores(d)

    def pass_v(d):
        if d < reach:

            @pl.when(has_up & (i >= d))
            def _():
                v_copy(d - 1).wait_recv()
                v_copy(d).start()

    def need_v(d):
        if d < reach:

            @pl.when(i + 1 >= ctx_n)
            def _():
                v_copy(d - 1).wait_recv()

        else:
            v_copy(d - 1).wait_recv()

    c_up.wait()
    acc = dot(wo_cut[t], gath[t], NN)
    if reach >= 1:
        take_k(1)
    ag_cross(0).wait_recv()
    ag_fwd(0).start()
    if reach >= 1:
        pass_v(1)
    for n in range(1, GATHER_PARTS):
        ag_cross(n).wait_recv()
        ag_fwd(n).start()
    for d in range(2, reach + 1):
        take_k(d)
        pass_v(d)
    ag_part.wait_recv()
    acc = acc + dot(wo_cut[partner], gath[partner], NN)
    acc = acc + dot(wo_cut[cross], gath[cross], NN)

    for d in range(1, reach + 1):

        @pl.when(i < d)
        def _():
            s[d] = jnp.full(s.shape[1:], NEG_FILL, F32)

    for g in range(kv_heads):
        top = jnp.max(s[0, g], axis=0, keepdims=True)
        for d in range(1, reach + 1):
            top = jnp.maximum(top, jnp.max(s[d, g], axis=0, keepdims=True))
        total = jnp.zeros((1, stacked), F32)
        for d in range(reach + 1):
            val = s[d, g]
            e = jnp.where(val > 0.5 * NEG_FILL, jnp.exp(val - top), 0.0)
            s[d, g] = e
            total = total + jnp.sum(e, axis=0, keepdims=True)
        inv_total = 1.0 / jnp.where(live[:1], total, 1.0)
        for d in range(reach + 1):
            s[d, g] = s[d, g] * inv_total

    for n in range(GATHER_PARTS):
        ag_fwd(n).wait_recv()
    acc = acc + dot(wo_cut[diag], gath[diag], NN)
    grad = acc.astype(BF)
    deltas = []
    for g in range(kv_heads):
        sums = []
        for r in range(group):
            h = g * group + r
            part = grad[head_cols(h)]
            do_t[g, :, r * rows : (r + 1) * rows] = part
            sums.append(
                jnp.sum(part.astype(F32) * ao_t[head_cols(h), :], axis=0, keepdims=True)
            )
        deltas.append(jnp.concatenate(sums, axis=1))

    def dk_copy(d):
        return remote(snd_k.at[d], rcv_k.at[d - 1], dk_s.at[d], dk_r.at[d - 1], down_dev)

    def dv_copy(d):
        return remote(snd_v.at[d], rcv_v.at[d - 1], dv_s.at[d], dv_r.at[d - 1], down_dev)

    dq[...] = jnp.zeros_like(dq)

    def first_of_chain(d):
        return i + 1 >= ctx_n if d < reach else i >= d

    def block(d):
        for g in range(kv_heads):
            part_v[d, :, head_cols(g)] = dot(s[d, g].astype(BF), do_t[g], NT)
        if d > 0:

            @pl.when(first_of_chain(d))
            def _():
                snd_v[d] = part_v[d].astype(BF)
                dv_copy(d).start()

            need_v(d)
        for g in range(kv_heads):
            dprob = dot(vb[d, :, head_cols(g)], do_t[g], NN)
            ds = (s[d, g] * (dprob - deltas[g])).astype(BF)
            part_k[d, :, head_cols(g)] = dot(ds, q_t[g], NT)
            dq[g] += dot(k_t[d, g], ds, NN)
        if d > 0:

            @pl.when(first_of_chain(d))
            def _():
                snd_k[d] = part_k[d].astype(BF)
                dk_copy(d).start()

    for d in range(reach, 0, -1):
        pl.when(i >= d)(functools.partial(block, d))
    c_v.wait()
    block(0)

    coupling = jnp.zeros((1, rows), F32)
    low = []
    for g in range(kv_heads):
        for r in range(group):
            cols = slice(r * rows, (r + 1) * rows)
            part = (dq[g, :, cols] * scale).astype(BF)
            low.append(part)
            coupling = coupling + jnp.sum(
                part.astype(F32) * q_t[g, :, cols].astype(F32), axis=0, keepdims=True
            )
    dq_low = jnp.concatenate(low, axis=0)
    owners = (diag, cross, partner, t)

    def piece_rows(n):
        return pl.ds(pl.multiple_of(owners[n] * width, 16), width)

    def query_piece(n):
        pacc[n] = dot(wq[piece_rows(n), :], dq_low, NN)

    c_wq.wait()
    done = 0
    for d in range(reach - 1, 0, -1):

        @pl.when(has_up & (i >= d))
        def _():
            dv_copy(d + 1).wait_recv()
            snd_v[d] = (part_v[d] + rcv_v[d].astype(F32)).astype(BF)
            dv_copy(d).start()
            dk_copy(d + 1).wait_recv()
            snd_k[d] = (part_k[d] + rcv_k[d].astype(F32)).astype(BF)
            dk_copy(d).start()

        if done < 4:
            query_piece(done)
            done += 1
    while done < 4:
        query_piece(done)
        done += 1
    c_wk.wait()
    c_wv.wait()
    c_xin.wait()
    c_inv.wait()
    if reach >= 1:

        @pl.when(has_up)
        def _():
            dv_copy(1).wait_recv()
            part_v[0] += rcv_v[0].astype(F32)

    dv_low = part_v[0].astype(BF)
    for n in range(4):
        pacc[n] += dot(wv[piece_rows(n), :], dv_low, NT)
    if reach >= 1:

        @pl.when(has_up)
        def _():
            dk_copy(1).wait_recv()
            part_k[0] += rcv_k[0].astype(F32)

    dk_low = (part_k[0] * scale).astype(BF)
    both = dk_low.astype(F32) * kb[0].astype(F32) + dv_low.astype(F32) * vb[0].astype(F32)
    for g in range(kv_heads):
        coupling = coupling + jnp.sum(both[:, head_cols(g)].T, axis=0, keepdims=True)

    def piece(n):
        return pacc[n] + dot(wk[piece_rows(n), :], dk_low, NT)

    lead = COUPLING_ROWS
    wide = jnp.broadcast_to(coupling, (lead, rows))

    send_a = remote(rs_a, rs_ar, rs_s.at[0], rs_rv.at[0], {"tp": partner})
    send_c = remote(rs_c, rs_cr, rs_s.at[1], rs_rv.at[1], {"tp": partner})

    def b_copy(n):
        sl = pl.ds(0, lead + chunk) if n == 0 else pl.ds(lead + n * chunk, chunk)
        return remote(
            rs_b.at[sl], rs_br.at[sl], rs_s.at[2 + n], rs_rv.at[2 + n], {"tp": cross}
        )

    def x_copy(n):
        sl = pl.ds(n * chunk, chunk)
        if pipe_n == 1:
            return pltpu.make_async_copy(res.at[sl], out_h.at[sl], x_s.at[n])
        return remote(res.at[sl], out_h.at[sl], x_s.at[n], x_r.at[n], {"pipe": prev})

    rs_a[lead:, :] = piece(0).astype(BF)
    rs_a[:lead, :] = wide.astype(BF)
    send_a.start()
    pacc[1] = piece(1)
    send_a.wait_recv()
    rs_b[:lead, :] = (wide + rs_ar[:lead, :].astype(F32)).astype(BF)
    for n in range(chunks):
        sl = slice(n * chunk, (n + 1) * chunk)
        sh = slice(lead + n * chunk, lead + (n + 1) * chunk)
        rs_b[sh, :] = (pacc[1, sl] + rs_ar[sh, :].astype(F32)).astype(BF)
        b_copy(n).start()
    rs_c[lead:, :] = piece(2).astype(BF)
    rs_c[:lead, :] = wide.astype(BF)
    send_c.start()
    pacc[3] = piece(3)
    iv = inv[...]
    send_c.wait_recv()
    for n in range(chunks):
        sl = slice(n * chunk, (n + 1) * chunk)
        sh = slice(lead + n * chunk, lead + (n + 1) * chunk)
        b_copy(n).wait_recv()
        if n == 0:
            coup = (
                coupling + rs_cr[:lead, :].astype(F32)[:1] + rs_br[:lead, :].astype(F32)[:1]
            )
            drag = iv * coup / model_width
        normed = pacc[3, sl] + rs_cr[sh, :].astype(F32) + rs_br[sh, :].astype(F32)
        val = gath[t, sl, :].astype(F32) + iv * (
            gain_col[sl, :] * normed - xin[sl, :].astype(F32) * drag
        )
        res[sl, :] = val.astype(BF)
        x_copy(n).start()

    for n in range(GATHER_PARTS):
        ag_cross(n).wait_send()
        ag_fwd(n).wait_send()
    ag_part.wait_send()
    for d in range(reach):

        @pl.when(has_up & (i >= d))
        def _():
            k_copy(d).wait_send()
            v_copy(d).wait_send()

    for d in range(1, reach + 1):

        @pl.when(i >= d)
        def _():
            dv_copy(d).wait_send()
            dk_copy(d).wait_send()

    send_a.wait_send()
    send_c.wait_send()
    for n in range(chunks):
        b_copy(n).wait_send()
    for n in range(chunks):
        x_copy(n).wait()


def per_device(up, xin, inv, gain, q, k, v, ao, wq, wk, wv, wo, lens):
    ctx_n = lax.axis_size("ctx")
    pipe_n = lax.axis_size("pipe")
    tp_n = lax.axis_size("tp")
    assert tp_n == 4
    up, xin, q, k, v, ao = up[0].T, xin[0].T, q[0], k[0], v[0], ao[0]
    wq, wk, wv, wo = wq[0], wk[0], wv[0], wo[0]
    width, rows = up.shape
    reach = min((WINDOW - 2 + rows) // rows, ctx_n - 1)
    kv_cols, q_cols = k.shape[1], q.shape[1]
    kv_heads = kv_cols // HEAD_SIZE
    stacked = rows * (q_cols // kv_cols)
    chunks = chunk_count(width)
    vm = pltpu.VMEM
    dma = pltpu.SemaphoreType.DMA
    blocks = reach + 1
    scratch = [
        vm((tp_n, width, rows), BF),
        vm((width, rows), BF),
        vm(inv.shape, F32),
        vm(gain.shape, F32),
        vm(q.shape, BF),
        vm((blocks, rows, kv_cols), BF),
        vm((blocks, rows, kv_cols), BF),
        vm(ao.shape, BF),
        vm(wq.shape, BF),
        vm(wk.shape, BF),
        vm(wv.shape, BF),
        vm(wo.shape, BF),
        pltpu.SMEM(lens.shape, jnp.int32),
        vm((tp_n, wo.shape[0], width), BF),
        vm((width, rows), F32),
        vm((q_cols, rows), F32),
        vm((kv_heads, HEAD_SIZE, stacked), BF),
        vm((blocks, kv_heads, HEAD_SIZE, rows), BF),
        vm((kv_heads, HEAD_SIZE, stacked), BF),
        vm((blocks, kv_heads, rows, stacked), F32),
        vm((blocks, rows, kv_cols), F32),
        vm((blocks, rows, kv_cols), F32),
        vm((blocks, rows, kv_cols), BF),
        vm((blocks, rows, kv_cols), BF),
        vm((blocks, rows, kv_cols), BF),
        vm((blocks, rows, kv_cols), BF),
        vm((kv_heads, HEAD_SIZE, stacked), F32),
        vm((tp_n, width, rows), F32),
    ]
    scratch += [vm((COUPLING_ROWS + width, rows), BF)] * 6
    scratch += [vm((width, rows), BF)]
    scratch += [dma((13,))]
    scratch += [dma((blocks,))] * 4
    scratch += [dma((2 * GATHER_PARTS + 1,))] * 2
    scratch += [dma((blocks,))] * 4
    scratch += [dma((2 + chunks,))] * 2
    scratch += [dma((chunks,))] * 2
    out = pl.pallas_call(
        functools.partial(kernel, ctx_n, pipe_n, reach),
        out_shape=jax.ShapeDtypeStruct((width, rows), BF),
        in_specs=[pl.BlockSpec(memory_space=pl.ANY)] * 13,
        out_specs=pl.BlockSpec(memory_space=pl.ANY),
        scratch_shapes=scratch,
        compiler_params=pltpu.CompilerParams(collective_id=0, has_side_effects=True),
        name="layer_backward",
    )(up, xin, inv, gain, q, k, v, ao, wq, wk, wv, wo, lens)
    return out.T[None]


def solution(mesh):
    placed = (
        P("pipe", "ctx", "tp"),
        P("pipe", "ctx", "tp"),
        P("pipe", "ctx"),
        P("pipe", "tp"),
        P("pipe", "ctx", "tp"),
        P("pipe", "ctx", "tp"),
        P("pipe", "ctx", "tp"),
        P("pipe", "ctx", "tp"),
        P("pipe", None, "tp"),
        P("pipe", None, "tp"),
        P("pipe", None, "tp"),
        P("pipe", "tp", None),
        P("pipe"),
    )
    return jax.shard_map(
        per_device, mesh=mesh, in_specs=placed, out_specs=P("pipe", "ctx", "tp"), check_vma=False
    )
```

time: 46.8 us -> 41.5 us (0.89)
  local copies, waits for them, and re-layouts: 5.19 us -> 1.6 us
  Pallas kernels: 40.7 us -> 39.1 us
    unnamed x2 -> x1, local copies, waits for them, and re-layouts: 3.46 us -> 1.6 us
    broadcast_in_dim x1 -> x0, local copies, waits for them, and re-layouts: 1.73 us -> none  [per_device(): return out[None]]
    pallas_call x1, Pallas kernels: 40.7 us -> 39.1 us  [per_device(): pl.pallas_call(functools.partial(kernel, ctx_n, pipe_n, reach), out_shape...]
where the time goes in v2:
time: 41.5 us; the launch traced here: 41.3 us
  Pallas kernels  39.1 us (94%)
  local copies, waits for them, and re-layouts  1.6 us (4%)
  between operations  0.66 us (2%)
    pallas_call x1, Pallas kernels, per_device(): pl.pallas_call(functools.partial(kernel, ctx_n, pipe_n, reach), out_shape...  39.1 us
    unnamed x1, local copies, waits for them, and re-layouts  1.6 us

profile of v2, /device:TPU:0, one launch (start us, length us, event | category | flops | bytes accessed | tf_op | source)
XLA Modules:
  0.0 41.3 jit_solution(12994502233158679127)
XLA Ops:
  0.7 39.1 %layer_backward.1 = bf16[672,128]{1,0:T(8,128)(2,1)} custom-call(bf16[672,128]{1,0:T(8,128)(2,1)} %bitcast.22, bf16[672,128]{1,0:T(8,128)(2,1)} %bitcast.23, f32[1,128]{1,0:T(1,128)} %inv_h.1, f32[1,672]{1,0:T(1,128)} %gain_h.1, bf16[128,512]{1,0:T(8,128)(2,1)} %bitcast.24, bf16[128,256]{1,0:T(8,128)(2,1)} %bitcast.26, bf16[128,256]{1,0:T(8,128)(2,1)} %bitcast.27, ...), custom_call_target="tpu_custom_call" | custom-call | tf_op jit(solution)/shard_map/layer_backward/pallas_call | solution.py:581
  39.7 1.6 %copy.16 = bf16[1,128,672]{1,2,0:T(8,128)(2,1)} copy(bf16[1,128,672]{1,2,0:T(8,128)(2,1)} %bitcast.21) | data formatting | bytes 344064

commit v3 on v2

--- a/solution.py
+++ b/solution.py
@@ -341,11 +341,15 @@
             )
         deltas.append(jnp.concatenate(sums, axis=1))
 
-    def dk_copy(d):
-        return remote(snd_k.at[d], rcv_k.at[d - 1], dk_s.at[d], dk_r.at[d - 1], down_dev)
-
-    def dv_copy(d):
-        return remote(snd_v.at[d], rcv_v.at[d - 1], dv_s.at[d], dv_r.at[d - 1], down_dev)
+    def dk_copy(d, g):
+        return remote(
+            snd_k.at[d, g], rcv_k.at[d - 1, g], dk_s.at[d, g], dk_r.at[d - 1, g], down_dev
+        )
+
+    def dv_copy(d, g):
+        return remote(
+            snd_v.at[d, g], rcv_v.at[d - 1, g], dv_s.at[d, g], dv_r.at[d - 1, g], down_dev
+        )
 
     dq[...] = jnp.zeros_like(dq)
 
@@ -354,26 +358,28 @@
 
     def block(d):
         for g in range(kv_heads):
-            part_v[d, :, head_cols(g)] = dot(s[d, g].astype(BF), do_t[g], NT)
+            part_v[d, g] = dot(s[d, g].astype(BF), do_t[g], NT)
+            if d > 0:
+
+                @pl.when(first_of_chain(d))
+                def _():
+                    snd_v[d, g] = part_v[d, g].astype(BF)
+                    dv_copy(d, g).start()
+
         if d > 0:
-
-            @pl.when(first_of_chain(d))
-            def _():
-                snd_v[d] = part_v[d].astype(BF)
-                dv_copy(d).start()
-
             need_v(d)
         for g in range(kv_heads):
             dprob = dot(vb[d, :, head_cols(g)], do_t[g], NN)
             ds = (s[d, g] * (dprob - deltas[g])).astype(BF)
-            part_k[d, :, head_cols(g)] = dot(ds, q_t[g], NT)
+            part_k[d, g] = dot(ds, q_t[g], NT)
+            if d > 0:
+
+                @pl.when(first_of_chain(d))
+                def _():
+                    snd_k[d, g] = part_k[d, g].astype(BF)
+                    dk_copy(d, g).start()
+
             dq[g] += dot(k_t[d, g], ds, NN)
-        if d > 0:
-
-            @pl.when(first_of_chain(d))
-            def _():
-                snd_k[d] = part_k[d].astype(BF)
-                dk_copy(d).start()
 
     for d in range(reach, 0, -1):
         pl.when(i >= d)(functools.partial(block, d))
@@ -405,12 +411,14 @@
 
         @pl.when(has_up & (i >= d))
         def _():
-            dv_copy(d + 1).wait_recv()
-            snd_v[d] = (part_v[d] + rcv_v[d].astype(F32)).astype(BF)
-            dv_copy(d).start()
-            dk_copy(d + 1).wait_recv()
-            snd_k[d] = (part_k[d] + rcv_k[d].astype(F32)).astype(BF)
-            dk_copy(d).start()
+            for g in range(kv_heads):
+                dv_copy(d + 1, g).wait_recv()
+                snd_v[d, g] = (part_v[d, g] + rcv_v[d, g].astype(F32)).astype(BF)
+                dv_copy(d, g).start()
+            for g in range(kv_heads):
+                dk_copy(d + 1, g).wait_recv()
+                snd_k[d, g] = (part_k[d, g] + rcv_k[d, g].astype(F32)).astype(BF)
+                dk_copy(d, g).start()
 
         if done < 4:
             query_piece(done)
@@ -426,20 +434,24 @@
 
         @pl.when(has_up)
         def _():
-            dv_copy(1).wait_recv()
-            part_v[0] += rcv_v[0].astype(F32)
-
-    dv_low = part_v[0].astype(BF)
+            for g in range(kv_heads):
+                dv_copy(1, g).wait_recv()
+                part_v[0, g] += rcv_v[0, g].astype(F32)
+
+    dv_low = jnp.concatenate([part_v[0, g].astype(BF) for g in range(kv_heads)], axis=1)
     for n in range(4):
         pacc[n] += dot(wv[piece_rows(n), :], dv_low, NT)
     if reach >= 1:
 
         @pl.when(has_up)
         def _():
-            dk_copy(1).wait_recv()
-            part_k[0] += rcv_k[0].astype(F32)
-
-    dk_low = (part_k[0] * scale).astype(BF)
+            for g in range(kv_heads):
+                dk_copy(1, g).wait_recv()
+                part_k[0, g] += rcv_k[0, g].astype(F32)
+
+    dk_low = jnp.concatenate(
+        [(part_k[0, g] * scale).astype(BF) for g in range(kv_heads)], axis=1
+    )
     both = dk_low.astype(F32) * kb[0].astype(F32) + dv_low.astype(F32) * vb[0].astype(F32)
     for g in range(kv_heads):
         coupling = coupling + jnp.sum(both[:, head_cols(g)].T, axis=0, keepdims=True)
@@ -513,8 +525,9 @@
 
         @pl.when(i >= d)
         def _():
-            dv_copy(d).wait_send()
-            dk_copy(d).wait_send()
+            for g in range(kv_heads):
+                dv_copy(d, g).wait_send()
+                dk_copy(d, g).wait_send()
 
     send_a.wait_send()
     send_c.wait_send()
@@ -561,12 +574,12 @@
         vm((blocks, kv_heads, HEAD_SIZE, rows), BF),
         vm((kv_heads, HEAD_SIZE, stacked), BF),
         vm((blocks, kv_heads, rows, stacked), F32),
-        vm((blocks, rows, kv_cols), F32),
-        vm((blocks, rows, kv_cols), F32),
-        vm((blocks, rows, kv_cols), BF),
-        vm((blocks, rows, kv_cols), BF),
-        vm((blocks, rows, kv_cols), BF),
-        vm((blocks, rows, kv_cols), BF),
+        vm((blocks, kv_heads, rows, HEAD_SIZE), F32),
+        vm((blocks, kv_heads, rows, HEAD_SIZE), F32),
+        vm((blocks, kv_heads, rows, HEAD_SIZE), BF),
+        vm((blocks, kv_heads, rows, HEAD_SIZE), BF),
+        vm((blocks, kv_heads, rows, HEAD_SIZE), BF),
+        vm((blocks, kv_heads, rows, HEAD_SIZE), BF),
         vm((kv_heads, HEAD_SIZE, stacked), F32),
         vm((tp_n, width, rows), F32),
     ]
@@ -575,7 +588,7 @@
     scratch += [dma((13,))]
     scratch += [dma((blocks,))] * 4
     scratch += [dma((2 * GATHER_PARTS + 1,))] * 2
-    scratch += [dma((blocks,))] * 4
+    scratch += [dma((blocks, kv_heads))] * 4
     scratch += [dma((2 + chunks,))] * 2
     scratch += [dma((chunks,))] * 2
     out = pl.pallas_call(

time: 41.5 us -> 40.9 us (0.986)
  Pallas kernels: 39.1 us -> 38.5 us
    pallas_call x1, Pallas kernels: 39.1 us -> 38.5 us  [per_device(): pl.pallas_call(functools.partial(kernel, ctx_n, pipe_n, reach), out_shape...]
where the time goes in v3:
time: 40.9 us; the launch traced here: 40.8 us
  Pallas kernels  38.5 us (94%)
  local copies, waits for them, and re-layouts  1.6 us (4%)
  between operations  0.66 us (2%)
    pallas_call x1, Pallas kernels, per_device(): pl.pallas_call(functools.partial(kernel, ctx_n, pipe_n, reach), out_shape...  38.5 us
    unnamed x1, local copies, waits for them, and re-layouts  1.6 us

profile of v3, /device:TPU:0, one launch (start us, length us, event | category | flops | bytes accessed | tf_op | source)
XLA Modules:
  0.0 40.8 jit_solution(3240978080324256485)
XLA Ops:
  0.7 38.5 %layer_backward.1 = bf16[672,128]{1,0:T(8,128)(2,1)} custom-call(bf16[672,128]{1,0:T(8,128)(2,1)} %bitcast.22, bf16[672,128]{1,0:T(8,128)(2,1)} %bitcast.23, f32[1,128]{1,0:T(1,128)} %inv_h.1, f32[1,672]{1,0:T(1,128)} %gain_h.1, bf16[128,512]{1,0:T(8,128)(2,1)} %bitcast.24, bf16[128,256]{1,0:T(8,128)(2,1)} %bitcast.26, bf16[128,256]{1,0:T(8,128)(2,1)} %bitcast.27, ...), custom_call_target="tpu_custom_call" | custom-call | tf_op jit(solution)/shard_map/layer_backward/pallas_call | solution.py:594
  39.2 1.6 %copy.16 = bf16[1,128,672]{1,2,0:T(8,128)(2,1)} copy(bf16[1,128,672]{1,2,0:T(8,128)(2,1)} %bitcast.21) | data formatting | bytes 344064

commit v4 on v3

--- a/solution.py
+++ b/solution.py
@@ -383,6 +383,20 @@
 
     for d in range(reach, 0, -1):
         pl.when(i >= d)(functools.partial(block, d))
+    def relay(d):
+        @pl.when(has_up & (i >= d))
+        def _():
+            for g in range(kv_heads):
+                dv_copy(d + 1, g).wait_recv()
+                snd_v[d, g] = (part_v[d, g] + rcv_v[d, g].astype(F32)).astype(BF)
+                dv_copy(d, g).start()
+            for g in range(kv_heads):
+                dk_copy(d + 1, g).wait_recv()
+                snd_k[d, g] = (part_k[d, g] + rcv_k[d, g].astype(F32)).astype(BF)
+                dk_copy(d, g).start()
+
+    if reach >= 2:
+        relay(reach - 1)
     c_v.wait()
     block(0)
 
@@ -409,17 +423,8 @@
     done = 0
     for d in range(reach - 1, 0, -1):
 
-        @pl.when(has_up & (i >= d))
-        def _():
-            for g in range(kv_heads):
-                dv_copy(d + 1, g).wait_recv()
-                snd_v[d, g] = (part_v[d, g] + rcv_v[d, g].astype(F32)).astype(BF)
-                dv_copy(d, g).start()
-            for g in range(kv_heads):
-                dk_copy(d + 1, g).wait_recv()
-                snd_k[d, g] = (part_k[d, g] + rcv_k[d, g].astype(F32)).astype(BF)
-                dk_copy(d, g).start()
-
+        if d < reach - 1:
+            relay(d)
         if done < 4:
             query_piece(done)
             done += 1

time: 40.9 us -> 40.9 us (level)
  no operation moved by 1% of the time
where the time goes in v4:
time: 40.9 us; the launch traced here: 40.8 us
  Pallas kernels  38.5 us (94%)
  local copies, waits for them, and re-layouts  1.6 us (4%)
  between operations  0.66 us (2%)
    pallas_call x1, Pallas kernels, per_device(): pl.pallas_call(functools.partial(kernel, ctx_n, pipe_n, reach), out_shape...  38.5 us
    unnamed x1, local copies, waits for them, and re-layouts  1.6 us

profile of v4, /device:TPU:0, one launch (start us, length us, event | category | flops | bytes accessed | tf_op | source)
XLA Modules:
  0.0 40.8 jit_solution(16764562899366240875)
XLA Ops:
  0.7 38.5 %layer_backward.1 = bf16[672,128]{1,0:T(8,128)(2,1)} custom-call(bf16[672,128]{1,0:T(8,128)(2,1)} %bitcast.22, bf16[672,128]{1,0:T(8,128)(2,1)} %bitcast.23, f32[1,128]{1,0:T(1,128)} %inv_h.1, f32[1,672]{1,0:T(1,128)} %gain_h.1, bf16[128,512]{1,0:T(8,128)(2,1)} %bitcast.24, bf16[128,256]{1,0:T(8,128)(2,1)} %bitcast.26, bf16[128,256]{1,0:T(8,128)(2,1)} %bitcast.27, ...), custom_call_target="tpu_custom_call" | custom-call | tf_op jit(solution)/shard_map/layer_backward/pallas_call | solution.py:599
  39.2 1.6 %copy.16 = bf16[1,128,672]{1,2,0:T(8,128)(2,1)} copy(bf16[1,128,672]{1,2,0:T(8,128)(2,1)} %bitcast.21) | data formatting | bytes 344064
